TPU v7x, 128 devices: a whole 4x4x4 slice. The times are simulated.
128 devices in a mesh: sample: 4 (over y_hi, core), turb: 32 (over x, y_lo, z).
Axes of the slice: x: 4, y: 4 (y_hi: 2, y_lo: 2; y = y_hi * 2 + y_lo), z: 4, core: 2. Of those that a mesh axis runs over, the one named last changes fastest.
Arguments:
- inflow: bfloat16 [32, 4096, 512], P('sample', 'turb'), may hold values from -6 to 6
- cotangent: bfloat16 [32, 4096, 512], P('sample', 'turb'), may hold values from -6 to 6
- norm_gain: float32 [512], replicated, may hold values from 0.25 to 1.75
- query_weight: bfloat16 [512, 512], replicated, may hold values from -2 to 2, as said below
- key_weight: bfloat16 [512, 512], replicated, may hold values from -2 to 2, as said below
- value_weight: bfloat16 [512, 512], replicated, may hold values from -0.25 to 0.25
- out_weight: bfloat16 [512, 512], replicated, may hold values from -0.25 to 0.25
- adjacency: int32 [8, 32, 3], replicated, may hold values from -1 to 31, as said below
- sectors: int32 [32], P('sample'), may hold values from 0 to 7, as said below
Outputs:
- layer_output: bfloat16 [32, 4096, 512], P('sample', 'turb')
- grad_inflow: bfloat16 [32, 4096, 512], P('sample', 'turb')
- grad_query_weight: float32 [512, 512], replicated
- grad_key_weight: float32 [512, 512], replicated
- grad_value_weight: float32 [512, 512], replicated
- grad_out_weight: float32 [512, 512], replicated
- grad_norm_gain: float32 [512], replicated
Inputs may be any that keep to these rules, and one draw needn't show every extreme that they name: `adjacency`: row [s, b] lists distinct blocks other than b, the used entries first and -1 after them. For every block and every group of 8 consecutive samples, another block is listed upstream of it for at most 1 of the group's samples, and some pair of blocks reaches 1. `sectors`: every group of 8 consecutive samples holds each sector exactly 1 times. `query_weight`: A projection of rows of 512 features. `key_weight`: A projection of rows of 512 features.
All inputs are finite; a program needn't handle non-finite values.
Results may differ from a plain program's by a relative error of at most 0.004.
The roundings to bfloat16 on the way count: a program that leaves them out, or rounds other values in their place, can miss the bound.
Values may be sent and summed in bfloat16 or wider, within the bound.
A program may use at most 192 MiB of HBM per device.

v0:
```python
import jax
import jax.numpy as jnp
from jax import lax
from jax.sharding import PartitionSpec as P

HEADS = 8
UPSTREAM = 3
SECTORS = 8
REPEAT = 1


epsilon = 1e-05


def normalize(row_block, norm_gain):
    widened = row_block.astype(jnp.float32)
    centred = widened - jnp.mean(widened, axis=-1, keepdims=True)
    inverse = lax.rsqrt(jnp.mean(centred * centred, axis=-1, keepdims=True) + epsilon)
    scaled = centred * inverse
    return (scaled, inverse, (scaled * norm_gain).astype(jnp.bfloat16))


def attend(pieces):
    queries, key_rows, value_rows, key_usable, grad_attended = pieces
    batch_count, query_count, model_width = queries.shape
    key_count = key_rows.shape[1]
    head_dim = model_width // HEADS
    score_scale = head_dim ** (-0.5)
    query_heads = queries.reshape(batch_count, query_count, HEADS, head_dim)
    key_heads = key_rows.reshape(batch_count, key_count, HEADS, head_dim)
    value_heads = value_rows.reshape(batch_count, key_count, HEADS, head_dim)
    grad_heads = grad_attended.reshape(batch_count, query_count, HEADS, head_dim)
    scores = (
        jnp.einsum("nqhd,nkhd->nhqk", query_heads, key_heads, preferred_element_type=jnp.float32)
        * score_scale
    )
    scores = jnp.where(key_usable[:, None, None, :], scores, -1e30)
    highest = jnp.max(scores, axis=-1, keepdims=True)
    weights = jnp.exp(scores - highest)
    probabilities = weights / jnp.sum(weights, axis=-1, keepdims=True)
    rounded = probabilities.astype(jnp.bfloat16)
    attended = jnp.einsum(
        "nhqk,nkhd->nqhd", rounded, value_heads, preferred_element_type=jnp.float32
    ).astype(jnp.bfloat16)
    grad_probs = jnp.einsum(
        "nqhd,nkhd->nhqk", grad_heads, value_heads, preferred_element_type=jnp.float32
    )
    centred = grad_probs - jnp.sum(probabilities * grad_probs, axis=-1, keepdims=True)
    grad_scores = (probabilities * centred * score_scale).astype(jnp.bfloat16)
    grad_queries = jnp.einsum(
        "nhqk,nkhd->nqhd", grad_scores, key_heads, preferred_element_type=jnp.float32
    ).astype(jnp.bfloat16)
    grad_keys = jnp.einsum(
        "nhqk,nqhd->nkhd", grad_scores, query_heads, preferred_element_type=jnp.float32
    )
    grad_values = jnp.einsum(
        "nhqk,nqhd->nkhd", rounded, grad_heads, preferred_element_type=jnp.float32
    )
    pair_terms = jnp.concatenate(
        [
            grad_keys.reshape(batch_count, key_count, model_width),
            grad_values.reshape(batch_count, key_count, model_width),
        ],
        axis=-1,
    )
    return (
        attended.reshape(batch_count, query_count, model_width),
        grad_queries.reshape(batch_count, query_count, model_width),
        pair_terms,
    )


def on_device(
    inflow,
    cotangent,
    norm_gain,
    query_weight,
    key_weight,
    value_weight,
    out_weight,
    adjacency,
    sectors,
):
    sample_count, block_rows, model_width = inflow.shape
    block_count = lax.axis_size("turb")
    own_block = lax.axis_index("turb")
    slot_count = REPEAT * ((SECTORS * UPSTREAM + block_count - 2) // (block_count - 1))
    flat_rows = sample_count * block_rows
    pair_width = 2 * model_width
    input_rows = inflow.reshape(flat_rows, model_width)
    grad_rows = cotangent.reshape(flat_rows, model_width)
    scaled, inverse, normed = normalize(input_rows, norm_gain)
    queries = jnp.dot(normed, query_weight, preferred_element_type=jnp.float32).astype(jnp.bfloat16)
    key_rows = jnp.dot(normed, key_weight, preferred_element_type=jnp.float32).astype(jnp.bfloat16)
    value_rows = jnp.dot(normed, value_weight, preferred_element_type=jnp.float32).astype(
        jnp.bfloat16
    )
    upstream = adjacency[sectors]
    needed = jnp.any(upstream == own_block, axis=2).astype(jnp.int32)
    earlier_need = jnp.cumsum(needed, axis=0) - needed
    slot_index = lax.broadcasted_iota(jnp.int32, (block_count, slot_count, sample_count), 1)
    chosen = (needed.T[:, None, :] == 1) & (earlier_need.T[:, None, :] == slot_index)
    selector = chosen.astype(jnp.bfloat16).reshape(block_count * slot_count, sample_count)
    own_lists = lax.dynamic_index_in_dim(upstream, own_block, axis=1, keepdims=False)
    usable = own_lists >= 0
    matches = jnp.any(own_lists[:, :, None, None] == own_lists[None, None, :, :], axis=3)
    sample_ids = lax.broadcasted_iota(jnp.int32, (sample_count, sample_count), 0)
    earlier = lax.broadcasted_iota(jnp.int32, (sample_count, sample_count), 1) < sample_ids
    position = jnp.sum((matches & earlier[:, None, :]).astype(jnp.int32), axis=2)
    flat_slot = own_lists * slot_count + position
    fetch_at = jnp.where(usable, flat_slot, 0)
    payload = jnp.concatenate([key_rows, value_rows], axis=1).reshape(
        sample_count, block_rows * pair_width
    )
    packed = jnp.dot(selector, payload, preferred_element_type=jnp.float32).astype(jnp.bfloat16)
    arrived = lax.all_to_all(
        packed.reshape(block_count, slot_count, block_rows, pair_width),
        "turb",
        split_axis=0,
        concat_axis=0,
        tiled=True,
    )
    fetched = arrived.reshape(block_count * slot_count, block_rows, pair_width)[fetch_at]
    upstream_keys = fetched[..., :model_width]
    upstream_values = fetched[..., model_width:]
    key_count = (1 + UPSTREAM) * block_rows
    key_all = jnp.concatenate(
        [key_rows.reshape(sample_count, 1, block_rows, model_width), upstream_keys], axis=1
    ).reshape(sample_count, key_count, model_width)
    value_all = jnp.concatenate(
        [value_rows.reshape(sample_count, 1, block_rows, model_width), upstream_values], axis=1
    ).reshape(sample_count, key_count, model_width)
    block_usable = jnp.concatenate([jnp.ones((sample_count, 1), dtype=jnp.bool_), usable], axis=1)
    key_usable = jnp.repeat(block_usable, block_rows, axis=1)
    grad_attended = jnp.dot(grad_rows, out_weight.T, preferred_element_type=jnp.float32).astype(
        jnp.bfloat16
    )
    group_size = min(sample_count, max(1, 512 // block_rows))
    while sample_count % group_size != 0:
        group_size = group_size - 1
    group_count = sample_count // group_size

    def grouped(tensor):
        return tensor.reshape((group_count, group_size) + tensor.shape[1:])

    attended, grad_queries, pair_terms = lax.map(
        attend,
        (
            grouped(queries.reshape(sample_count, block_rows, model_width)),
            grouped(key_all),
            grouped(value_all),
            grouped(key_usable),
            grouped(grad_attended.reshape(sample_count, block_rows, model_width)),
        ),
    )
    attended = attended.reshape(flat_rows, model_width)
    grad_queries = grad_queries.reshape(flat_rows, model_width)
    pair_terms = pair_terms.reshape(sample_count, 1 + UPSTREAM, block_rows, pair_width)
    layer_output = (
        (
            input_rows.astype(jnp.float32)
            + jnp.dot(attended, out_weight, preferred_element_type=jnp.float32)
        )
        .astype(jnp.bfloat16)
        .reshape(inflow.shape)
    )
    outgoing = (
        pair_terms[:, 1:]
        .astype(jnp.bfloat16)
        .reshape(sample_count * UPSTREAM, block_rows, pair_width)
    )
    target = jnp.where(usable, flat_slot, block_count * slot_count).reshape(-1)
    outbound = (
        jnp.zeros((block_count * slot_count, block_rows, pair_width), jnp.bfloat16)
        .at[target]
        .set(outgoing, mode="drop")
    )
    sum_out = jnp.dot(attended.T, grad_rows, preferred_element_type=jnp.float32)
    sum_query = jnp.dot(normed.T, grad_queries, preferred_element_type=jnp.float32)
    returned = lax.all_to_all(
        outbound.reshape(block_count, slot_count, block_rows, pair_width),
        "turb",
        split_axis=0,
        concat_axis=0,
        tiled=True,
    )
    remote = jnp.dot(
        selector.T,
        returned.reshape(block_count * slot_count, block_rows * pair_width),
        preferred_element_type=jnp.float32,
    )
    combined = (
        (pair_terms[:, 0].reshape(sample_count, block_rows * pair_width) + remote)
        .astype(jnp.bfloat16)
        .reshape(flat_rows, pair_width)
    )
    grad_keys = combined[:, :model_width]
    grad_values = combined[:, model_width:]
    sum_key = jnp.dot(normed.T, grad_keys, preferred_element_type=jnp.float32)
    sum_value = jnp.dot(normed.T, grad_values, preferred_element_type=jnp.float32)
    grad_normed = jnp.dot(grad_queries, query_weight.T, preferred_element_type=jnp.float32)
    grad_normed = grad_normed + jnp.dot(grad_keys, key_weight.T, preferred_element_type=jnp.float32)
    grad_normed = grad_normed + jnp.dot(
        grad_values, value_weight.T, preferred_element_type=jnp.float32
    )
    sum_gain = jnp.sum(grad_normed * scaled, axis=0)
    grad_scaled = grad_normed * norm_gain
    grad_input = inverse * (
        grad_scaled
        - jnp.mean(grad_scaled, axis=-1, keepdims=True)
        - scaled * jnp.mean(grad_scaled * scaled, axis=-1, keepdims=True)
    )
    grad_inflow = (
        (grad_rows.astype(jnp.float32) + grad_input).astype(jnp.bfloat16).reshape(inflow.shape)
    )
    sum_query, sum_key, sum_value, sum_out, sum_gain = lax.psum(
        (sum_query, sum_key, sum_value, sum_out, sum_gain), ("sample", "turb")
    )
    return (layer_output, grad_inflow, sum_query, sum_key, sum_value, sum_out, sum_gain)


def solution(mesh):
    placed = (
        P("sample", "turb", None),
        P("sample", "turb", None),
        P(),
        P(),
        P(),
        P(),
        P(),
        P(),
        P("sample"),
    )
    return jax.shard_map(
        on_device,
        mesh=mesh,
        in_specs=placed,
        out_specs=(P("sample", "turb", None), P("sample", "turb", None), P(), P(), P(), P(), P()),
        check_vma=False,
    )
```

profile of v0, /device:TPU:1, one launch (start us, length us, event | category | flops | bytes accessed | tf_op | source)
XLA Modules:
  0.0 828.1 jit_solution(11748716253074594821)
XLA Ops:
  20.8 7.2 convolution_convert_fusion
  28.0 11.3 %copy.96 = bf16[4,8,128,1024]{3,2,1,0:T(8,128)(2,1)} copy(bf16[4,8,128,1024]{3,1,2,0:T(8,128)(2,1)} %bitcast.179) | data formatting | bytes 16777216
  39.4 10.3 %all-to-all-start = ((bf16[32,1,128,1024]{3,2,1,0:T(8,128)(2,1)}), bf16[32,1,128,1024]{3,2,1,0:T(8,128)(2,1)}, u32[]{:S(2)}, u32[]{:S(2)}) async-start(bf16[32,1,128,1024]{3,2,1,0:T(8,128)(2,1)} %bitcast.178), calls=%async_computation | async-start | bytes 16777216 | tf_op jit(solution)/shard_map/all_to_all | solution.py:116
  53.3 2.8 convolution_convert_fusion.1
  56.0 106.5 %all-to-all-done = bf16[32,1,128,1024]{3,2,1,0:T(8,128)(2,1)} async-done(((bf16[32,1,128,1024]{3,2,1,0:T(8,128)(2,1)}), bf16[32,1,128,1024]{3,2,1,0:T(8,128)(2,1)}, u32[]{:S(2)}, u32[]{:S(2)}) %all-to-all-start) | async-done | bytes 8388640 | tf_op jit(solution)/shard_map/all_to_all | solution.py:116
  162.6 7.8 gather_fusion.1
  170.4 3.5 fusion.65
  173.9 3.6 pad_maximum_fusion
  177.5 276.7 %while.14 = (s32[]{:T(128)}, bf16[2,4,128,512]{3,2,1,0:T(8,128)(2,1)}, bf16[2,4,128,512]{3,2,1,0:T(8,128)(2,1)}, f32[2,4,512,1024]{3,2,1,0:T(8,128)}, bf16[2,4,5...) while((s32[]{:T(128)}, ...), condition=%wide.region_10.11_spmd, body=%wide.region_6.10_spmd.sunk | while | flops 1659381248 | bytes 168908992 | solution.py:146
  183.0 3.1 constant_dynamic-slice_fusion.12
  186.0 2.8 copy.111
  188.8 4.5 fusion.134
  196.2 7.8 fusion.135
  204.1 34.5 %fusion.136 = bf16[4,8,64,128]{3,2,1,0:T(8,128)(2,1)} fusion(bf16[4,512,8,64]{1,3,2,0:T(8,128)(2,1)} %bitcast.174, f32[4,8,128,512]{3,2,1,0:T(8,128)} %fusion.134, f32[4,8,128,512]{3,2,1,0:T(8,128)} %get-tuple-element.194, f32[4,8,128]{2,1,0:T(8,128)S(1)} %get-tuple-element.195), kind=kOutput, calls=%fused_computation.23.clone.1 | convolution fusion | flops 283382272 | bytes 19415040 | tf_op jit(solution)/shard_map/while/body/eval_jaxpr/nhqk,nkhd->nqhd/dot_general | solution.py:50
  240.6 5.8 fusion.137
  249.8 6.2 fusion.138
  256.0 35.0 %fusion.139 = f32[4,8,64,512]{3,2,1,0:T(8,128)} fusion(bf16[4,128,8,64]{1,3,2,0:T(8,128)(2,1)S(1)} %bitcast.184, f32[4,8,128,512]{3,2,1,0:T(8,128)} %fusion.134, f32[4,8,128,512]{3,2,1,0:T(8,128)} %get-tuple-element.194, f32[4,8,128]{2,1,0:T(8,128)S(1)} %get-tuple-element.195), kind=kOutput, calls=%fused_computation.15.clone.1 | convolution fusion | flops 283120128 | bytes 21512192 | tf_op jit(solution)/shard_map/while/body/eval_jaxpr/nhqk,nqhd->nkhd/dot_general | solution.py:53
  291.0 7.7 maximum_bitcast_fusion.2
  298.6 8.7 %copy.115 = f32[1,4,512,1024]{3,2,1,0:T(8,128)} copy(f32[1,4,512,1024]{2,3,1,0:T(8,128)} %maximum_bitcast_fusion.2) | data formatting | bytes 16777216 | tf_op jit(solution)/shard_map/while/body/jit(dynamic_update_index_in_dim)/dynamic_update_slice | solution.py:146
  307.4 8.3 constant_dynamic-update-slice_fusion.6
  321.1 3.1 constant_dynamic-slice_fusion.12
  324.2 2.8 copy.111
  327.0 4.5 fusion.134
  334.4 7.8 fusion.135
  342.2 34.5 %fusion.136 = bf16[4,8,64,128]{3,2,1,0:T(8,128)(2,1)} fusion(bf16[4,512,8,64]{1,3,2,0:T(8,128)(2,1)} %bitcast.174, f32[4,8,128,512]{3,2,1,0:T(8,128)} %fusion.134, f32[4,8,128,512]{3,2,1,0:T(8,128)} %get-tuple-element.194, f32[4,8,128]{2,1,0:T(8,128)S(1)} %get-tuple-element.195), kind=kOutput, calls=%fused_computation.23.clone.1 | convolution fusion | flops 283382272 | bytes 19415040 | tf_op jit(solution)/shard_map/while/body/eval_jaxpr/nhqk,nkhd->nqhd/dot_general | solution.py:50
  378.8 5.8 fusion.137
  388.0 6.2 fusion.138
  394.2 35.0 %fusion.139 = f32[4,8,64,512]{3,2,1,0:T(8,128)} fusion(bf16[4,128,8,64]{1,3,2,0:T(8,128)(2,1)S(1)} %bitcast.184, f32[4,8,128,512]{3,2,1,0:T(8,128)} %fusion.134, f32[4,8,128,512]{3,2,1,0:T(8,128)} %get-tuple-element.194, f32[4,8,128]{2,1,0:T(8,128)S(1)} %get-tuple-element.195), kind=kOutput, calls=%fused_computation.15.clone.1 | convolution fusion | flops 283120128 | bytes 21512192 | tf_op jit(solution)/shard_map/while/body/eval_jaxpr/nhqk,nqhd->nkhd/dot_general | solution.py:53
  429.1 7.7 maximum_bitcast_fusion.2
  436.8 8.7 %copy.115 = f32[1,4,512,1024]{3,2,1,0:T(8,128)} copy(f32[1,4,512,1024]{2,3,1,0:T(8,128)} %maximum_bitcast_fusion.2) | data formatting | bytes 16777216 | tf_op jit(solution)/shard_map/while/body/jit(dynamic_update_index_in_dim)/dynamic_update_slice | solution.py:146
  445.5 8.3 constant_dynamic-update-slice_fusion.6
  454.2 8.2 slice.45
  462.4 4.3 broadcast_in_dim.60
  466.7 13.0 %scatter_fusion = bf16[32,128,1024]{2,1,0:T(8,128)(2,1)} fusion(bf16[32,128,1024]{2,1,0:T(8,128)(2,1)} %broadcast_in_dim.60, s32[24]{0:T(128)S(1)} %copy-done.32, bf16[24,128,1024]{2,1,0:T(8,128)(2,1)} %bitcast.181), kind=kCustom, calls=%fused_computation.2 | custom fusion | bytes 18874464 | tf_op jit(solution)/shard_map/scatter | solution.py:176
  479.7 21.0 %all-to-all-start.1 = ((bf16[32,1,128,1024]{3,2,1,0:T(8,128)(2,1)}), bf16[32,1,128,1024]{3,2,1,0:T(8,128)(2,1)}, u32[]{:S(2)}, u32[]{:S(2)}) async-start(bf16[32,1,128,1024]{3,2,1,0:T(8,128)(2,1)} %bitcast.172), calls=%async_computation.1 | async-start | bytes 16777216 | tf_op jit(solution)/shard_map/all_to_all | solution.py:180
  501.2 2.5 slice_bitcast_fusion
  503.7 4.4 copy.97
  511.6 100.1 %all-to-all-done.1 = bf16[32,1,128,1024]{3,2,1,0:T(8,128)(2,1)} async-done(((bf16[32,1,128,1024]{3,2,1,0:T(8,128)(2,1)}), bf16[32,1,128,1024]{3,2,1,0:T(8,128)(2,1)}, u32[]{:S(2)}, u32[]{:S(2)}) %all-to-all-start.1) | async-done | bytes 8388640 | tf_op jit(solution)/shard_map/all_to_all | solution.py:180
  611.6 11.4 %copy.98 = bf16[4,8,128,1024]{3,1,2,0:T(8,128)(2,1)} copy(bf16[4,8,128,1024]{3,2,1,0:T(8,128)(2,1)} %bitcast.56) | data formatting | bytes 16777216
  623.1 7.1 fusion.33
  630.2 3.9 reshape.254
  634.1 3.4 fusion.55
  641.6 3.0 fusion.51
  645.4 2.9 fusion.50
  648.3 86.8 %psum.39 = f32[512]{0:T(512)} all-reduce(f32[512]{0:T(512)S(1)} %get-tuple-element.95), channel_id=1, replica_groups=mesh['sample'=4,'turb'=32] {'sample','turb'}, use_global_device_ids=true, to_apply=%region_19.20 | all-reduce | flops 512 | bytes 4096 | tf_op jit(solution)/shard_map/psum | solution.py:216
  735.1 2.9 fusion.49
  738.0 76.5 %all-reduce.4.cloned.1.call-done = (f32[512,512]{1,0:T(8,128)}, f32[512,512]{1,0:T(8,128)}, f32[512,512]{1,0:T(8,128)}, f32[512,512]{1,0:T(8,128)}) async-done(((f32[512,512]{1,0:T(8,128)}, f32[512,512]{1,0:T(8,128)}, f32[512,512]{1,0:T(8,128)}, f32[512,512]{1,0:T(8,128)}), (f32[512,512]{1,0:T(8,128)}, f32[512,512]{1,0:T(8,128)}, f32[512,512]{1,0:T(8,128)}, ...) | async-done | bytes 4194320 | tf_op jit(solution)/shard_map/psum | solution.py:216
  814.5 2.4 copy.138
  (143 shorter events, 57.6 us)
Async XLA Ops:
  7.2 8.1 copy-start
  7.9 8.4 %copy-start.20 = (bf16[512,512]{1,0:T(8,128)(2,1)S(1)}, bf16[512,512]{1,0:T(8,128)(2,1)}, u32[]{:S(2)}) copy-start(bf16[512,512]{1,0:T(8,128)(2,1)} %param.15) | copy-start | bytes 1572868
  9.3 11.5 %copy-start.30 = (pred[8,32]{1,0:T(8,128)(4,1)}, pred[8,32]{1,0:T(8,128)(4,1)S(1)}, u32[]{:S(2)}) copy-start(pred[8,32]{1,0:T(8,128)(4,1)S(1)} %fusion.59) | copy-start | bytes 772
  10.8 0.6 copy-start.26
  10.8 5.2 copy-start.22
  13.7 2.4 copy-start.24
  15.3 1.0 copy-start.13
  16.3 1.0 copy-start.6
  17.3 1.0 copy-start.8
  39.4 12.2 %copy-start.14 = (bf16[1024,512]{1,0:T(8,128)(2,1)S(1)}, bf16[1024,512]{1,0:T(8,128)(2,1)}, u32[]{:S(2)}) copy-start(bf16[1024,512]{1,0:T(8,128)(2,1)} %copy-done.13) | copy-start | bytes 3145732
  39.4 12.2 %copy-start.18 = (bf16[512,512]{1,0:T(8,128)(2,1)S(1)}, bf16[512,512]{1,0:T(8,128)(2,1)}, u32[]{:S(2)}) copy-start(bf16[512,512]{1,0:T(8,128)(2,1)} %param.14) | copy-start | bytes 1572868
  39.4 13.9 %copy-start.10 = (bf16[8,128,512]{2,1,0:T(8,128)(2,1)S(1)}, bf16[8,128,512]{2,1,0:T(8,128)(2,1)}, u32[]{:S(2)}) copy-start(bf16[8,128,512]{2,1,0:T(8,128)(2,1)} %param.12) | copy-start | bytes 3145732
  39.4 123.2 %all-to-all-start = ((bf16[32,1,128,1024]{3,2,1,0:T(8,128)(2,1)}), bf16[32,1,128,1024]{3,2,1,0:T(8,128)(2,1)}, u32[]{:S(2)}, u32[]{:S(2)}) async-start(bf16[32,1,128,1024]{3,2,1,0:T(8,128)(2,1)} %bitcast.178), calls=%async_computation | async-start | bytes 16777216 | tf_op jit(solution)/shard_map/all_to_all | solution.py:116
  170.4 3.5 copy-start.7
  170.4 3.5 copy-start.9
  188.8 4.5 copy-start.5
  249.8 6.2 copy-start.2
  327.0 4.5 copy-start.5
  388.0 6.2 copy-start.2
  462.4 4.3 copy-start.32
  479.7 21.1 %copy-start.1 = (bf16[8,128,512]{2,1,0:T(8,128)(2,1)S(1)}, bf16[8,128,512]{2,1,0:T(8,128)(2,1)}, u32[]{:S(2)}) copy-start(bf16[8,128,512]{2,1,0:T(8,128)(2,1)} %param.11) | copy-start | bytes 3145732
  479.7 21.1 %copy-start.27 = (f32[8,128]{1,0:T(8,128)S(1)}, f32[8,128]{1,0:T(8,128)}, u32[]{:S(2)}) copy-start(f32[8,128]{1,0:T(8,128)} %copy-done.26) | copy-start | bytes 12292
  479.7 21.1 %copy-start.28 = (f32[512]{0:T(512)S(1)}, f32[512]{0:T(512)}, u32[]{:S(2)}) copy-start(f32[512]{0:T(512)} %param.13) | copy-start | bytes 6148
  479.7 21.1 %copy-start.29 = (f32[8,128]{1,0:T(8,128)S(1)}, f32[8,128]{1,0:T(8,128)}, u32[]{:S(2)}) copy-start(f32[8,128]{1,0:T(8,128)} %get-tuple-element.128) | copy-start | bytes 12292
  479.7 131.9 %all-to-all-start.1 = ((bf16[32,1,128,1024]{3,2,1,0:T(8,128)(2,1)}), bf16[32,1,128,1024]{3,2,1,0:T(8,128)(2,1)}, u32[]{:S(2)}, u32[]{:S(2)}) async-start(bf16[32,1,128,1024]{3,2,1,0:T(8,128)(2,1)} %bitcast.172), calls=%async_computation.1 | async-start | bytes 16777216 | tf_op jit(solution)/shard_map/all_to_all | solution.py:180
  500.7 313.8 %all-reduce.4.cloned.1.call-start = ((), (), s32[]{:S(2)}) async-start(), calls=%async_computation.2 | async-start | bytes 8388608 | tf_op jit(solution)/shard_map/psum | solution.py:216
  503.7 4.4 copy-start.11
  503.7 4.4 copy-start.33
  508.1 1.7 copy-start.12
  611.6 11.4 %copy-start.31 = (pred[8,32]{1,0:T(8,128)(4,1)S(1)}, pred[8,32]{1,0:T(8,128)(4,1)}, u32[]{:S(2)}) copy-start(pred[8,32]{1,0:T(8,128)(4,1)} %copy-done.30) | copy-start | bytes 772
  634.1 3.4 copy-start.3
  634.1 3.4 copy-start.15
  637.5 1.9 copy-start.19
  639.4 5.2 copy-start.4
  639.4 5.2 copy-start.21
  641.5 3.8 copy-start.23
  641.6 3.8 copy-start.25
  814.5 4.7 copy-start.17
  814.5 5.7 copy-start.16
Sparse Core Ops, SparseCore 0:
  639.5 174.9 all-reduce.3
where the time goes:
time: 838 us; the launch traced here: 828 us
  waiting for transfers between devices  283 us (34%)
  matrix products  225 us (27%)
  local copies, waits for them, and re-layouts  157 us (19%)
  blocking collectives  86.8 us (10%)
  starting transfers between devices  31.3 us (4%)
  other arithmetic  29.5 us (4%)
  between operations  14.7 us (2%)
    all_to_all x1, waiting for transfers between devices, on_device(): lax.all_to_all(packed.reshape(block_count, slot_count, block_rows, pair_w...  107 us
    all_to_all x1, waiting for transfers between devices, on_device(): lax.all_to_all(outbound.reshape(block_count, slot_count, block_rows, pair...  100 us
    psum x1, blocking collectives, on_device(): lax.psum((sum_query, sum_key, sum_value, sum_out, sum_gain), ('sample', '...  86.8 us
    psum x1, waiting for transfers between devices, on_device(): lax.psum((sum_query, sum_key, sum_value, sum_out, sum_gain), ('sample', '...  76.5 us
    dot_general x2, matrix products, attend(): jnp.einsum('nhqk,nqhd->nkhd', grad_scores, query_heads, preferred_element...  69.9 us
    dot_general x2, matrix products, attend(): jnp.einsum('nhqk,nkhd->nqhd', grad_scores, key_heads, preferred_element_t...  69 us
    dynamic_update_slice x10, local copies, waits for them, and re-layouts, on_device(): lax.map(attend, (grouped(queries.reshape(sample_count, block_rows, model_...  44.8 us
    unnamed x73, local copies, waits for them, and re-layouts  38.5 us
  transfers between devices with their start and end apart: 3, of which 3 were waited for; matrix products, arithmetic and copies ran while one was open for 3% of the time, Pallas kernels for 0%

commit v1 on v0

v1 whole, which is shorter than its diff:
```python
import jax
import jax.numpy as jnp
from jax import lax
from jax.experimental import pallas as pl
from jax.experimental.pallas import tpu as pltpu
from jax.sharding import PartitionSpec as P

F32 = jnp.float32
BF16 = jnp.bfloat16
HEADS = 8
UPSTREAM = 3
EPSILON = 1e-05
VMEM_BYTES = 56 << 20


def dot(a, b):
    return jnp.dot(a, b, preferred_element_type=F32)


def dot_nt(a, b):
    return lax.dot_general(a, b, (((1,), (1,)), ((), ())), preferred_element_type=F32)


def whole(*shape):
    return pl.BlockSpec(shape, lambda *_: (0,) * len(shape))


def row_statistics(rows):
    widened = rows.astype(F32)
    centred = widened - jnp.mean(widened, axis=-1, keepdims=True)
    inverse = lax.rsqrt(jnp.mean(centred * centred, axis=-1, keepdims=True) + EPSILON)
    return centred * inverse, inverse


def normalize_and_pack(chosen_ref, inflow_ref, gain_ref, normed_ref, packed_ref):
    for s in range(inflow_ref.shape[0]):
        scaled, _ = row_statistics(inflow_ref[s])
        normed_ref[s] = (scaled * gain_ref[...]).astype(BF16)

    @pl.loop(0, packed_ref.shape[0])
    def _(d):
        packed_ref[d] = normed_ref[chosen_ref[d]]


def attend(
    order_ref,
    source_ref,
    target_ref,
    count_ref,
    own_ref,
    inflow_ref,
    cotangent_ref,
    up0_ref,
    up1_ref,
    up2_ref,
    wq_ref,
    wkv_ref,
    wkv_t_ref,
    wq_t_ref,
    wo_ref,
    wo_t_ref,
    out_ref,
    grad_own_ref,
    sent_ref,
    gw_ref,
    x_ref,
    kv_ref,
    kvt_ref,
    dkv_ref,
    att_t_ref,
    dq_t_ref,
):
    step = pl.program_id(0)
    block, width = own_ref.shape[1], own_ref.shape[2]
    pair = 2 * (width // HEADS)
    used = count_ref[step]

    @pl.when(step == 0)
    def _():
        gw_ref[...] = jnp.zeros_like(gw_ref)

    own = own_ref[0]
    cot = cotangent_ref[0]
    x_ref[0:block] = own
    for u, ref in enumerate((up0_ref, up1_ref, up2_ref)):
        x_ref[(u + 1) * block : (u + 2) * block] = ref[0]
    x = x_ref[...]
    kv_ref[...] = dot(x, wkv_ref[...]).astype(BF16)
    kvt_ref[...] = dot_nt(wkv_t_ref[...], x).astype(BF16)
    queries = (dot(own, wq_ref[...]).astype(BF16).astype(F32) * 0.125).astype(BF16)
    grads = dot(cot, wo_t_ref[...]).astype(BF16)
    lane = lax.broadcasted_iota(jnp.int32, (block, pair), 1) < pair // 2
    sub = lax.broadcasted_iota(jnp.int32, (pair, block), 0) < pair // 2
    zero = jnp.zeros((block, pair), BF16)
    bias = [jnp.where(u < used, 0.0, -1e30).astype(F32) for u in range(UPSTREAM)]

    def spread(rows):
        return jnp.concatenate([jnp.where(lane, rows, zero), jnp.where(lane, zero, rows)], axis=0)

    for p in range(width // pair):
        lo, hi = p * pair, (p + 1) * pair
        q_pair = spread(queries[:, lo:hi])
        g_pair = spread(grads[:, lo:hi])
        scores = dot_nt(kv_ref[:, lo:hi], q_pair)
        scores = jnp.concatenate(
            [scores[0:block]]
            + [scores[(u + 1) * block : (u + 2) * block] + bias[u] for u in range(UPSTREAM)],
            axis=0,
        )
        highest = jnp.max(scores, axis=0, keepdims=True)
        weights = jnp.exp(scores - highest)
        probs = weights * (1.0 / jnp.sum(weights, axis=0, keepdims=True))
        rounded = probs.astype(BF16)
        grad_probs = dot_nt(kv_ref[:, width + lo : width + hi], g_pair)
        centre = jnp.sum(probs * grad_probs, axis=0, keepdims=True)
        grad_scores = (probs * (grad_probs - centre)).astype(BF16)
        dkv_ref[:, width + lo : width + hi] = dot(rounded, g_pair).astype(BF16)
        dkv_ref[:, lo:hi] = dot(grad_scores, q_pair).astype(BF16)
        both = dot(kvt_ref[width + lo : width + hi, :], rounded)
        att_t_ref[lo:hi, :] = jnp.where(sub, both[:, :block], both[:, block:]).astype(BF16)
        both = dot(kvt_ref[lo:hi, :], grad_scores) * 0.125
        dq_t_ref[lo:hi, :] = jnp.where(sub, both[:, :block], both[:, block:]).astype(BF16)

    attended = att_t_ref[...].T
    dq = dq_t_ref[...].T
    out_ref[0] = (inflow_ref[0].astype(F32) + dot(attended, wo_ref[...])).astype(BF16)
    back = dot(dkv_ref[...], wkv_t_ref[...])
    grad_own_ref[0] = back[0:block] + dot(dq, wq_t_ref[...])
    for u in range(UPSTREAM):
        sent_ref[target_ref[UPSTREAM * step + u]] = back[
            (u + 1) * block : (u + 2) * block
        ].astype(BF16)
    x_t = x.T
    gw_ref[0] += dot(x_t[:, 0:block], dq)
    gw_kv = dot(x_t, dkv_ref[...])
    gw_ref[1] += gw_kv[:, :width]
    gw_ref[2] += gw_kv[:, width:]
    gw_ref[3] += dot(att_t_ref[...], cot)


def finish(
    chosen_ref, wanted_ref, grad_own_ref, returned_ref, inflow_ref, cotangent_ref, gain_ref, out_ref, sum_ref
):
    sum_ref[...] = grad_own_ref[...]

    @pl.loop(0, returned_ref.shape[0])
    def _(d):
        @pl.when(wanted_ref[d] > 0)
        def _():
            s = chosen_ref[d]
            sum_ref[s] = sum_ref[s] + returned_ref[d].astype(F32)

    for s in range(inflow_ref.shape[0]):
        scaled, inverse = row_statistics(inflow_ref[s])
        grad_scaled = sum_ref[s] * gain_ref[...]
        grad_input = inverse * (
            grad_scaled
            - jnp.mean(grad_scaled, axis=-1, keepdims=True)
            - scaled * jnp.mean(grad_scaled * scaled, axis=-1, keepdims=True)
        )
        out_ref[s] = (cotangent_ref[s].astype(F32) + grad_input).astype(BF16)


def on_device(
    inflow, cotangent, norm_gain, query_weight, key_weight, value_weight, out_weight, adjacency, sectors
):
    samples, block, width = inflow.shape
    blocks = lax.axis_size("turb")
    me = lax.axis_index("turb")
    gain = norm_gain.reshape(1, width)
    sample_ids = lax.broadcasted_iota(jnp.int32, (samples, samples), 0)
    sector_ids = lax.broadcasted_iota(jnp.int32, (samples, samples), 1)
    order = jnp.sum(jnp.where(sectors[:, None] == sector_ids, sample_ids, 0), axis=0)
    lists_me = adjacency == me
    chosen = jnp.sum(jnp.where(lists_me, order[:, None, None], 0), axis=(0, 2))
    wanted = jnp.sum(lists_me.astype(jnp.int32), axis=(0, 2))
    own_lists = lax.dynamic_index_in_dim(adjacency, me, axis=1, keepdims=False)
    usable = own_lists >= 0
    count = jnp.sum(usable.astype(jnp.int32), axis=1)
    spare = jnp.where(me == 0, 1, 0)
    source = jnp.where(usable, own_lists, spare).reshape(-1)
    target = jnp.where(usable, own_lists, me).reshape(-1)

    rows = jax.ShapeDtypeStruct((samples, block, width), BF16)
    buffer = jax.ShapeDtypeStruct((blocks, block, width), BF16)
    normed, packed = pl.pallas_call(
        normalize_and_pack,
        out_shape=(rows, buffer),
        grid_spec=pltpu.PrefetchScalarGridSpec(
            num_scalar_prefetch=1,
            grid=(1,),
            in_specs=[whole(*inflow.shape), whole(1, width)],
            out_specs=[whole(*rows.shape), whole(*buffer.shape)],
        ),
        compiler_params=pltpu.CompilerParams(vmem_limit_bytes=VMEM_BYTES),
    )(chosen, inflow, gain)
    arrived = lax.all_to_all(packed, "turb", split_axis=0, concat_axis=0, tiled=True)

    wkv = jnp.concatenate([key_weight, value_weight], axis=1)

    def sample_block(index):
        return pl.BlockSpec((1, block, width), lambda i, o, s, t, c: (o[i], 0, 0))

    def up_block(u):
        return pl.BlockSpec((1, block, width), lambda i, o, s, t, c: (s[UPSTREAM * i + u], 0, 0))

    layer_output, grad_own, sent, gw = pl.pallas_call(
        attend,
        out_shape=(
            rows,
            jax.ShapeDtypeStruct((samples, block, width), F32),
            buffer,
            jax.ShapeDtypeStruct((4, width, width), F32),
        ),
        grid_spec=pltpu.PrefetchScalarGridSpec(
            num_scalar_prefetch=4,
            grid=(samples,),
            in_specs=[sample_block(0)] * 3
            + [up_block(u) for u in range(UPSTREAM)]
            + [
                whole(width, width),
                whole(width, 2 * width),
                whole(2 * width, width),
                whole(width, width),
                whole(width, width),
                whole(width, width),
            ],
            out_specs=[
                sample_block(0),
                sample_block(0),
                whole(*buffer.shape),
                whole(4, width, width),
            ],
            scratch_shapes=[
                pltpu.VMEM(((1 + UPSTREAM) * block, width), BF16),
                pltpu.VMEM(((1 + UPSTREAM) * block, 2 * width), BF16),
                pltpu.VMEM((2 * width, (1 + UPSTREAM) * block), BF16),
                pltpu.VMEM(((1 + UPSTREAM) * block, 2 * width), BF16),
                pltpu.VMEM((width, block), BF16),
                pltpu.VMEM((width, block), BF16),
            ],
        ),
        compiler_params=pltpu.CompilerParams(vmem_limit_bytes=VMEM_BYTES),
    )(
        order,
        source,
        target,
        count,
        normed,
        inflow,
        cotangent,
        arrived,
        arrived,
        arrived,
        query_weight,
        wkv,
        wkv.T,
        query_weight.T,
        out_weight,
        out_weight.T,
    )
    returned = lax.all_to_all(sent, "turb", split_axis=0, concat_axis=0, tiled=True)
    grad_inflow = pl.pallas_call(
        finish,
        out_shape=rows,
        grid_spec=pltpu.PrefetchScalarGridSpec(
            num_scalar_prefetch=2,
            grid=(1,),
            in_specs=[
                whole(samples, block, width),
                whole(*buffer.shape),
                whole(*inflow.shape),
                whole(*inflow.shape),
                whole(1, width),
            ],
            out_specs=whole(*rows.shape),
            scratch_shapes=[pltpu.VMEM((samples, block, width), F32)],
        ),
        compiler_params=pltpu.CompilerParams(vmem_limit_bytes=VMEM_BYTES),
    )(chosen, wanted, grad_own, returned, inflow, cotangent, gain)
    gw = lax.psum(gw, ("sample", "turb"))
    weighted = (
        query_weight.astype(F32) * gw[0]
        + key_weight.astype(F32) * gw[1]
        + value_weight.astype(F32) * gw[2]
    )
    gain_grad = jnp.sum(weighted, axis=1) / norm_gain
    return (layer_output, grad_inflow, gw[0], gw[1], gw[2], gw[3], gain_grad)


def solution(mesh):
    placed = (
        P("sample", "turb", None),
        P("sample", "turb", None),
        P(),
        P(),
        P(),
        P(),
        P(),
        P(),
        P("sample"),
    )
    return jax.shard_map(
        on_device,
        mesh=mesh,
        in_specs=placed,
        out_specs=(P("sample", "turb", None), P("sample", "turb", None), P(), P(), P(), P(), P()),
        check_vma=False,
    )
```

time: 838 us -> 351 us (0.42); the launches traced: 828 us -> 351 us
  matrix products: 225 us -> 0 us
  local copies, waits for them, and re-layouts: 157 us -> 6.25 us
  blocking collectives: 86.8 us -> 0 us
  Pallas kernels: 0 us -> 65.6 us
  waiting for transfers between devices: 283 us -> 241 us
  other arithmetic: 29.5 us -> 8.94 us
  starting transfers between devices: 31.3 us -> 15.7 us
    dot_general x24 -> x0, matrix products: 210 us -> none  [the longest x2 69.9 us: attend(): jnp.einsum('nhqk,nqhd->nkhd', grad_scores, query_heads, preferred_element...]
    all_to_all x2, waiting for transfers between devices: 207 us -> 48.7 us  [the longest x1 48.7 us: on_device(): lax.all_to_all(packed, 'turb', split_axis=0, concat_axis=0, tiled=True)]
    psum x1, waiting for transfers between devices: 76.5 us -> 191 us  [on_device(): gw = lax.psum(gw, ('sample', 'turb'))]
    psum x1 -> x0, blocking collectives: 86.8 us -> none  [on_device(): lax.psum((sum_query, sum_key, sum_value, sum_out, sum_gain), ('sample', '...]
    pallas_call x0 -> x3, Pallas kernels: none -> 65.6 us  [the longest x1 52.9 us: on_device(): pl.pallas_call(attend, out_shape=(rows, jax.ShapeDtypeStruct((samples, bl...]
    dynamic_update_slice x10 -> x0, local copies, waits for them, and re-layouts: 44.8 us -> none  [on_device(): lax.map(attend, (grouped(queries.reshape(sample_count, block_rows, model_...]
    unnamed x73 -> x20, local copies, waits for them, and re-layouts: 38.5 us -> 2.47 us
    dynamic_slice x18 -> x1, local copies, waits for them, and re-layouts: 28.7 us -> 0.13 us  [on_device(): own_lists = lax.dynamic_index_in_dim(adjacency, me, axis=1, keepdims=False)]
  transfers between devices with their start and end apart: 3 -> 3, of which waited for: 3 -> 2; matrix products, arithmetic and copies ran while one was open for 3% -> 4% of each run, Pallas kernels for 0% -> 0%
where the time goes in v1:
time: 351 us
  waiting for transfers between devices  241 us (69%)
  Pallas kernels  65.6 us (19%)
  starting transfers between devices  15.7 us (4%)
  between operations  14.1 us (4%)
  other arithmetic  8.94 us (3%)
  local copies, waits for them, and re-layouts  6.25 us (2%)
    psum x1, waiting for transfers between devices, on_device(): gw = lax.psum(gw, ('sample', 'turb'))  191 us
    pallas_call x1, Pallas kernels, on_device(): pl.pallas_call(attend, out_shape=(rows, jax.ShapeDtypeStruct((samples, bl...  52.9 us
    all_to_all x1, waiting for transfers between devices, on_device(): lax.all_to_all(packed, 'turb', split_axis=0, concat_axis=0, tiled=True)  48.7 us
    all_to_all x1, starting transfers between devices, on_device(): lax.all_to_all(packed, 'turb', split_axis=0, concat_axis=0, tiled=True)  10 us
    pallas_call x1, Pallas kernels, on_device(): pl.pallas_call(finish, out_shape=rows, grid_spec=pltpu.PrefetchScalarGrid...  7.39 us
  transfers between devices with their start and end apart: 3, of which 2 were waited for; matrix products, arithmetic and copies ran while one was open for 4% of the time, Pallas kernels for 0%

profile of v1, /device:TPU:1, one launch (start us, length us, event | category | flops | bytes accessed | tf_op | source)
XLA Modules:
  0.0 351.1 jit_solution(2130113573156548195)
XLA Ops:
  7.2 0.7 select_reduce_fusion.1.order_ref
  7.9 0.0 copy-start.7
  7.9 1.4 convert_reduce_fusion
  9.3 5.3 %shard_map.144 = (bf16[8,128,512]{2,1,0:T(8,128)(2,1)}, bf16[32,128,512]{2,1,0:T(8,128)(2,1)}) custom-call(s32[32]{0:T(128)} %get-tuple-element.20.chosen_ref, bf16[8,128,512]{2,1,0:T(8,128)(2,1)} %inflow_ref.5, f32[1,512]{1,0:T(1,128)} %bitcast.20), custom_call_target="tpu_custom_call" | custom-call | tf_op jit(solution)/shard_map/pallas_call | solution.py:186
  14.6 0.0 copy-start.5
  14.6 0.0 copy-start.4
  14.7 0.0 copy-start.3
  14.7 0.0 copy-start.2
  14.7 0.0 copy-start
  14.7 0.0 copy-done.7
  14.7 10.0 %all-to-all-start = ((bf16[32,128,512]{2,1,0:T(8,128)(2,1)}), bf16[32,128,512]{2,1,0:T(8,128)(2,1)}, u32[]{:S(2)}, u32[]{:S(2)}) async-start(bf16[32,128,512]{2,1,0:T(8,128)(2,1)} %get-tuple-element.14), calls=%async_computation | async-start | bytes 8388608 | tf_op jit(solution)/shard_map/all_to_all | solution.py:197
  24.7 0.0 copy-done.5
  24.7 0.7 convert_reduce_fusion.1
  25.4 0.1 copy.28
  25.6 0.1 squeeze.19
  25.6 0.0 copy-done.4
  25.6 0.2 copy.29
  25.9 0.0 copy-done.3
  25.9 0.2 copy.30
  26.1 0.0 copy-done.2
  26.1 1.0 copy.32
  27.1 0.0 copy-done
  27.1 1.0 copy.31
  28.1 1.1 fusion
  29.2 1.3 copy.33.wkv_ref
  30.5 0.6 compare_select_fusion
  31.1 48.7 %all-to-all-done.up0_ref.up1_ref.up2_ref = bf16[32,128,512]{2,1,0:T(8,128)(2,1)} async-done(((bf16[32,128,512]{2,1,0:T(8,128)(2,1)}), bf16[32,128,512]{2,1,0:T(8,128)(2,1)}, u32[]{:S(2)}, u32[]{:S(2)}) %all-to-all-start) | async-done | bytes 4194336 | tf_op jit(solution)/shard_map/all_to_all | solution.py:197
  79.8 52.9 %shard_map.145 = (bf16[8,128,512]{2,1,0:T(8,128)(2,1)}, f32[8,128,512]{2,1,0:T(8,128)}, bf16[32,128,512]{2,1,0:T(8,128)(2,1)}, f32[4,512,512]{2,1,0:T(8,128)}) custom-call(s32[8]{0:T(128)} %copy-done.7, s32[24]{0:T(128)} %get-tuple-element.30.source_ref, s32[24]{0:T(128)} %get-tuple-element.29.target_ref, s32[8]{0:T(128)} %get-tuple-element.25.count_ref, ...), custom_call_target="tpu_custom_call" | custom-call | tf_op jit(solution)/shard_map/pallas_call | solution.py:207
  132.7 5.6 %all-to-all-start.1 = ((bf16[32,128,512]{2,1,0:T(8,128)(2,1)}), bf16[32,128,512]{2,1,0:T(8,128)(2,1)}, u32[]{:S(2)}, u32[]{:S(2)}) async-start(bf16[32,128,512]{2,1,0:T(8,128)(2,1)} %get-tuple-element.17), calls=%async_computation.1 | async-start | bytes 8388608 | tf_op jit(solution)/shard_map/all_to_all | solution.py:262
  138.3 0.0 copy-start.1
  138.3 0.0 all-reduce.2.cloned.1.call-start
  138.4 0.7 all-reduce.2.cloned.1.call-update
  139.1 0.0 copy-start.6
  139.1 191.1 %all-reduce.2.cloned.1.call-done = f32[4,512,512]{2,1,0:T(8,128)} async-done(((f32[4,512,512]{2,1,0:T(8,128)}), f32[4,512,512]{2,1,0:T(8,128)}) %all-reduce.2.cloned.1.call-update) | async-done | bytes 4194320 | tf_op jit(solution)/shard_map/psum | solution.py:281
  330.2 0.0 copy-done.1
  330.2 3.8 %add_reduce_fusion = (f32[512]{0:T(512)S(1)}, f32[512,512]{1,0:T(8,128)}, f32[512,512]{1,0:T(8,128)}, f32[512,512]{1,0:T(8,128)}) fusion(bf16[512,512]{1,0:T(8,128)(2,1)S(1)} %copy-done.3, bf16[512,512]{1,0:T(8,128)(2,1)S(1)} %copy-done.4, bf16[512,512]{1,0:T(8,128)(2,1)S(1)} %copy-done.1, f32[4,512,512]{2,1,0:T(8,128)} %all-reduce.2.cloned.1.call-done), kind=kLoop, calls=%fused_computation.5 | loop fusion | flops 2358784 | bytes 7866368 | tf_op jit(solution)/shard_map/reduce_sum | solution.py:287
  334.0 0.0 copy-done.6
  334.0 0.6 div.3
  334.6 2.3 slice_bitcast_fusion
  336.9 0.0 all-to-all-done.1.returned_ref
  336.9 7.4 %shard_map.146 = bf16[8,128,512]{2,1,0:T(8,128)(2,1)} custom-call(s32[32]{0:T(128)} %get-tuple-element.20.chosen_ref, s32[32]{0:T(128)} %get-tuple-element.19.wanted_ref, f32[8,128,512]{2,1,0:T(8,128)} %get-tuple-element.16.grad_own_ref, bf16[32,128,512]{2,1,0:T(8,128)(2,1)} %all-to-all-done.1.returned_ref, bf16[8,128,512]{2,1,0:T(8,128)(2,1)} %inflow_ref.5, ...), custom_call_target="tpu_custom_call" | custom-call | tf_op jit(solution)/shard_map/pallas_call | solution.py:263
Async XLA Ops:
  7.9 6.8 %copy-start.7 = (s32[8]{0:T(128)}, s32[8]{0:T(128)S(1)}, u32[]{:S(2)}) copy-start(s32[8]{0:T(128)S(1)} %select_reduce_fusion.1.order_ref) | copy-start | bytes 100
  14.6 10.1 %copy-start.5 = (s32[8,32,3]{1,0,2:T(8,128)S(1)}, s32[8,32,3]{1,0,2:T(8,128)}, u32[]{:S(2)}) copy-start(s32[8,32,3]{1,0,2:T(8,128)} %param.16) | copy-start | bytes 9220
  14.6 11.0 %copy-start.4 = (bf16[512,512]{1,0:T(8,128)(2,1)S(1)}, bf16[512,512]{1,0:T(8,128)(2,1)}, u32[]{:S(2)}) copy-start(bf16[512,512]{1,0:T(8,128)(2,1)} %param.13) | copy-start | bytes 1572868
  14.7 11.2 %copy-start.3 = (bf16[512,512]{1,0:T(8,128)(2,1)S(1)}, bf16[512,512]{1,0:T(8,128)(2,1)}, u32[]{:S(2)}) copy-start(bf16[512,512]{1,0:T(8,128)(2,1)} %param.14) | copy-start | bytes 1572868
  14.7 11.4 %copy-start.2 = (bf16[512,512]{1,0:T(8,128)(2,1)S(1)}, bf16[512,512]{1,0:T(8,128)(2,1)}, u32[]{:S(2)}) copy-start(bf16[512,512]{1,0:T(8,128)(2,1)} %wo_ref.1) | copy-start | bytes 1572868
  14.7 12.4 %copy-start = (bf16[512,512]{1,0:T(8,128)(2,1)S(1)}, bf16[512,512]{1,0:T(8,128)(2,1)}, u32[]{:S(2)}) copy-start(bf16[512,512]{1,0:T(8,128)(2,1)} %wq_ref.1) | copy-start | bytes 1572868
  14.7 65.1 %all-to-all-start = ((bf16[32,128,512]{2,1,0:T(8,128)(2,1)}), bf16[32,128,512]{2,1,0:T(8,128)(2,1)}, u32[]{:S(2)}, u32[]{:S(2)}) async-start(bf16[32,128,512]{2,1,0:T(8,128)(2,1)} %get-tuple-element.14), calls=%async_computation | async-start | bytes 8388608 | tf_op jit(solution)/shard_map/all_to_all | solution.py:197
  132.7 204.2 %all-to-all-start.1 = ((bf16[32,128,512]{2,1,0:T(8,128)(2,1)}), bf16[32,128,512]{2,1,0:T(8,128)(2,1)}, u32[]{:S(2)}, u32[]{:S(2)}) async-start(bf16[32,128,512]{2,1,0:T(8,128)(2,1)} %get-tuple-element.17), calls=%async_computation.1 | async-start | bytes 8388608 | tf_op jit(solution)/shard_map/all_to_all | solution.py:262
  138.3 191.9 %copy-start.1 = (bf16[512,512]{1,0:T(8,128)(2,1)S(1)}, bf16[512,512]{1,0:T(8,128)(2,1)}, u32[]{:S(2)}) copy-start(bf16[512,512]{1,0:T(8,128)(2,1)} %wq_ref.1) | copy-start | bytes 1572868
  138.3 191.9 %all-reduce.2.cloned.1.call-start = ((), (), s32[]{:S(2)}) async-start(), calls=%async_computation.2 | async-start | bytes 8388608 | tf_op jit(solution)/shard_map/psum | solution.py:281
  139.1 194.9 %copy-start.6 = (f32[512]{0:T(512)S(1)}, f32[512]{0:T(512)}, u32[]{:S(2)}) copy-start(f32[512]{0:T(512)} %param.11) | copy-start | bytes 6148
Sparse Core Ops, SparseCore 0:
  144.1 186.0 all-reduce.1

commit v2 on v1

--- a/solution.py
+++ b/solution.py
@@ -11,6 +11,8 @@
 UPSTREAM = 3
 EPSILON = 1e-05
 VMEM_BYTES = 56 << 20
+MESH = pl.DeviceIdType.MESH
+BACK = (1, 9, 15, 19, 23, 27)
 
 
 def dot(a, b):
@@ -159,6 +161,264 @@
             - scaled * jnp.mean(grad_scaled * scaled, axis=-1, keepdims=True)
         )
         out_ref[s] = (cotangent_ref[s].astype(F32) + grad_input).astype(BF16)
+
+
+def exchange(
+    sent_ref,
+    gw_ref,
+    returned_ref,
+    total_ref,
+    half_ref,
+    core_in_ref,
+    a1_in_ref,
+    b1_in_ref,
+    a2_in_ref,
+    b2_in_ref,
+    a1_ref,
+    b1_ref,
+    last_ref,
+    last_in_ref,
+    local_sem,
+    back_send,
+    back_recv,
+    core_send,
+    core_recv,
+    a_send,
+    a_recv,
+    b_send,
+    b_recv,
+):
+    sample = lax.axis_index("sample")
+    turb = lax.axis_index("turb")
+    core = lax.rem(sample, 2)
+    high = sample - core
+    x, yz = turb // 8, lax.rem(turb, 8)
+    half = half_ref.shape[0]
+    x_rows, yz_rows, last_rows = a1_ref.shape[0], b1_ref.shape[0], last_ref.shape[0] // 2
+    color = half // 2
+
+    def at_turb(k):
+        return {"turb": turb ^ k}
+
+    partner = {"sample": high + 1 - core}
+    across = {"sample": lax.rem(sample + 2, 4)}
+
+    barrier = pltpu.get_barrier_semaphore()
+    pl.semaphore_signal(barrier, inc=1, device_id=partner, device_id_type=MESH)
+    pl.semaphore_signal(barrier, inc=1, device_id=across, device_id_type=MESH)
+
+    @pl.loop(1, 32)
+    def _(k):
+        pl.semaphore_signal(barrier, inc=1, device_id=at_turb(k), device_id_type=MESH)
+
+    pl.semaphore_wait(barrier, 33)
+
+    def remote(source, target, send, recv, device):
+        return pltpu.make_async_remote_copy(
+            src_ref=source,
+            dst_ref=target,
+            send_sem=send,
+            recv_sem=recv,
+            device_id=device,
+            device_id_type=MESH,
+        )
+
+    def back(k):
+        return remote(
+            sent_ref.at[turb ^ k], returned_ref.at[turb], back_send.at[k], back_recv.at[k], at_turb(k)
+        )
+
+    def start_back(low, high):
+        @pl.loop(low, high)
+        def _(k):
+            back(k).start()
+
+    def rows(ref, start, count):
+        return ref.at[pl.ds(pl.multiple_of(start, 8), count)]
+
+    def start_all(copies):
+        for c in copies:
+            c.start()
+
+    def wait_all(copies):
+        for c in copies:
+            c.wait()
+
+    own_half = pltpu.make_async_copy(rows(gw_ref, core * half, half), half_ref, local_sem.at[0])
+    own_half.start()
+    fold = remote(
+        rows(gw_ref, (1 - core) * half, half), core_in_ref, core_send.at[0], core_recv.at[0], partner
+    )
+    fold.start()
+    start_back(BACK[0], BACK[1])
+    own_half.wait()
+    fold.wait()
+    half_ref[...] = half_ref[...] + core_in_ref[...]
+
+    over_x = [
+        remote(
+            rows(half_ref, (x ^ k) * x_rows, x_rows),
+            a1_in_ref.at[k],
+            a_send.at[0, k],
+            a_recv.at[0, k],
+            at_turb(8 * k),
+        )
+        for k in range(1, 4)
+    ]
+    over_yz = [
+        remote(
+            rows(half_ref, color + (yz ^ k) * yz_rows, yz_rows),
+            b1_in_ref.at[k],
+            b_send.at[0, k],
+            b_recv.at[0, k],
+            at_turb(k),
+        )
+        for k in range(1, 8)
+    ]
+    start_all(over_x + over_yz)
+    start_back(BACK[1], BACK[2])
+    wait_all(over_x)
+    a1_ref[...] = (
+        half_ref[pl.ds(pl.multiple_of(x * x_rows, 8), x_rows), :]
+        + a1_in_ref[1]
+        + a1_in_ref[2]
+        + a1_in_ref[3]
+    )
+    second_a = [
+        remote(
+            rows(a1_ref, (yz ^ k) * last_rows, last_rows),
+            a2_in_ref.at[k],
+            a_send.at[1, k],
+            a_recv.at[1, k],
+            at_turb(k),
+        )
+        for k in range(1, 8)
+    ]
+    start_all(second_a)
+    wait_all(over_yz)
+    b1 = half_ref[pl.ds(pl.multiple_of(color + yz * yz_rows, 8), yz_rows), :]
+    for k in range(1, 8):
+        b1 = b1 + b1_in_ref[k]
+    b1_ref[...] = b1
+    second_b = [
+        remote(
+            rows(b1_ref, (x ^ k) * last_rows, last_rows),
+            b2_in_ref.at[k],
+            b_send.at[1, k],
+            b_recv.at[1, k],
+            at_turb(8 * k),
+        )
+        for k in range(1, 4)
+    ]
+    start_all(second_b)
+    start_back(BACK[2], BACK[3])
+    wait_all(second_a)
+    a2 = a1_ref[pl.ds(pl.multiple_of(yz * last_rows, 8), last_rows), :]
+    for k in range(1, 8):
+        a2 = a2 + a2_in_ref[k]
+    last_ref[0:last_rows] = a2
+    wait_all(second_b)
+    b2 = b1_ref[pl.ds(pl.multiple_of(x * last_rows, 8), last_rows), :]
+    for k in range(1, 4):
+        b2 = b2 + b2_in_ref[k]
+    last_ref[last_rows : 2 * last_rows] = b2
+    swap = remote(last_ref, last_in_ref, core_send.at[1], core_recv.at[1], across)
+    swap.start()
+    start_back(BACK[3], BACK[4])
+    swap.wait()
+    last_ref[...] = last_ref[...] + last_in_ref[...]
+
+    a_row = core * half + x * x_rows
+    b_row = core * half + color + yz * yz_rows
+    a_last = rows(total_ref, a_row + yz * last_rows, last_rows)
+    b_last = rows(total_ref, b_row + x * last_rows, last_rows)
+    keep_a = pltpu.make_async_copy(last_ref.at[0:last_rows], a_last, local_sem.at[1])
+    keep_b = pltpu.make_async_copy(last_ref.at[last_rows : 2 * last_rows], b_last, local_sem.at[2])
+    gather_a = [
+        remote(last_ref.at[0:last_rows], a_last, a_send.at[2, k], a_recv.at[2, k], at_turb(k))
+        for k in range(1, 8)
+    ]
+    gather_b = [
+        remote(
+            last_ref.at[last_rows : 2 * last_rows],
+            b_last,
+            b_send.at[2, k],
+            b_recv.at[2, k],
+            at_turb(8 * k),
+        )
+        for k in range(1, 4)
+    ]
+    start_all([keep_a, keep_b] + gather_a + gather_b)
+    start_back(BACK[4], BACK[5])
+    wait_all([keep_a] + gather_a)
+    a_part = rows(total_ref, a_row, x_rows)
+    spread_a = [
+        remote(a_part, a_part, a_send.at[3, k], a_recv.at[3, k], at_turb(8 * k)) for k in range(1, 4)
+    ]
+    start_all(spread_a)
+    wait_all([keep_b] + gather_b)
+    b_part = rows(total_ref, b_row, yz_rows)
+    spread_b = [
+        remote(b_part, b_part, b_send.at[3, k], b_recv.at[3, k], at_turb(k)) for k in range(1, 8)
+    ]
+    start_all(spread_b)
+    start_back(BACK[5], 32)
+    wait_all(spread_a)
+    a_half = rows(total_ref, core * half, color)
+    share_a = remote(a_half, a_half, core_send.at[2], core_recv.at[2], partner)
+    share_a.start()
+    wait_all(spread_b)
+    b_half = rows(total_ref, core * half + color, color)
+    share_b = remote(b_half, b_half, core_send.at[3], core_recv.at[3], partner)
+    share_b.start()
+
+    @pl.loop(1, 32)
+    def _(k):
+        back(k).wait()
+
+    share_a.wait()
+    share_b.wait()
+
+
+def exchange_gradients(sent, gw):
+    total_rows, width = gw.shape
+    half = total_rows // 2
+    x_rows, yz_rows, last_rows = half // 8, half // 16, half // 64
+    anywhere = pl.BlockSpec(memory_space=pl.ANY)
+    dma = pltpu.SemaphoreType.DMA
+    return pl.pallas_call(
+        exchange,
+        out_shape=(
+            jax.ShapeDtypeStruct(sent.shape, sent.dtype),
+            jax.ShapeDtypeStruct(gw.shape, gw.dtype),
+        ),
+        in_specs=[anywhere, anywhere],
+        out_specs=[anywhere, anywhere],
+        scratch_shapes=[
+            pltpu.VMEM((half, width), F32),
+            pltpu.VMEM((half, width), F32),
+            pltpu.VMEM((4, x_rows, width), F32),
+            pltpu.VMEM((8, yz_rows, width), F32),
+            pltpu.VMEM((8, last_rows, width), F32),
+            pltpu.VMEM((4, last_rows, width), F32),
+            pltpu.VMEM((x_rows, width), F32),
+            pltpu.VMEM((yz_rows, width), F32),
+            pltpu.VMEM((2 * last_rows, width), F32),
+            pltpu.VMEM((2 * last_rows, width), F32),
+            dma((3,)),
+            dma((32,)),
+            dma((32,)),
+            dma((4,)),
+            dma((4,)),
+            dma((4, 8)),
+            dma((4, 8)),
+            dma((4, 8)),
+            dma((4, 8)),
+        ],
+        compiler_params=pltpu.CompilerParams(
+            vmem_limit_bytes=VMEM_BYTES, collective_id=0, has_side_effects=True
+        ),
+    )(sent, gw)
 
 
 def on_device(
@@ -259,7 +519,7 @@
         out_weight,
         out_weight.T,
     )
-    returned = lax.all_to_all(sent, "turb", split_axis=0, concat_axis=0, tiled=True)
+    returned, gw = exchange_gradients(sent, gw.reshape(4 * width, width))
     grad_inflow = pl.pallas_call(
         finish,
         out_shape=rows,
@@ -278,7 +538,7 @@
         ),
         compiler_params=pltpu.CompilerParams(vmem_limit_bytes=VMEM_BYTES),
     )(chosen, wanted, grad_own, returned, inflow, cotangent, gain)
-    gw = lax.psum(gw, ("sample", "turb"))
+    gw = gw.reshape(4, width, width)
     weighted = (
         query_weight.astype(F32) * gw[0]
         + key_weight.astype(F32) * gw[1]

time: 351 us -> 254 us (0.72)
  waiting for transfers between devices: 241 us -> 48.7 us
  Pallas kernels: 65.6 us -> 180 us
  between operations: 14.1 us -> 0.77 us
  starting transfers between devices: 15.7 us -> 10 us
    psum x1 -> x0, waiting for transfers between devices: 191 us -> none  [on_device(): gw = lax.psum(gw, ('sample', 'turb'))]
    pallas_call x0 -> x1, Pallas kernels: none -> 114 us  [exchange_gradients(): pl.pallas_call(exchange, out_shape=(jax.ShapeDtypeStruct(sent.shape, sent...]
    all_to_all x1 -> x0, starting transfers between devices: 5.61 us -> none  [on_device(): lax.all_to_all(sent, 'turb', split_axis=0, concat_axis=0, tiled=True)]
  transfers between devices with their start and end apart: 3 -> 1, of which waited for: 2 -> 1; matrix products, arithmetic and copies ran while one was open for 4% -> 3% of each run, Pallas kernels for 0% -> 0%
where the time goes in v2:
time: 254 us; the launch traced here: 253 us
  Pallas kernels  180 us (71%)
  waiting for transfers between devices  48.7 us (19%)
  starting transfers between devices  10 us (4%)
  other arithmetic  9.61 us (4%)
  local copies, waits for them, and re-layouts  4 us (2%)
    pallas_call x1, Pallas kernels, exchange_gradients(): pl.pallas_call(exchange, out_shape=(jax.ShapeDtypeStruct(sent.shape, sent...  114 us
    pallas_call x1, Pallas kernels, on_device(): pl.pallas_call(attend, out_shape=(rows, jax.ShapeDtypeStruct((samples, bl...  52.9 us
    all_to_all x1, waiting for transfers between devices, on_device(): lax.all_to_all(packed, 'turb', split_axis=0, concat_axis=0, tiled=True)  48.7 us
    all_to_all x1, starting transfers between devices, on_device(): lax.all_to_all(packed, 'turb', split_axis=0, concat_axis=0, tiled=True)  10 us
    pallas_call x1, Pallas kernels, on_device(): pl.pallas_call(finish, out_shape=rows, grid_spec=pltpu.PrefetchScalarGrid...  7.45 us
    pallas_call x1, Pallas kernels, on_device(): pl.pallas_call(normalize_and_pack, out_shape=(rows, buffer), grid_spec=pl...  5.35 us
  transfers between devices with their start and end apart: 1, of which 1 were waited for; matrix products, arithmetic and copies ran while one was open for 3% of the time, Pallas kernels for 0%

profile of v2, /device:TPU:1, one launch (start us, length us, event | category | flops | bytes accessed | tf_op | source)
XLA Modules:
  0.0 252.6 jit_solution(4688850907775537822)
XLA Ops:
  0.6 0.7 select_reduce_fusion.1.order_ref
  1.4 0.0 copy-start.8
  1.4 1.4 convert_reduce_fusion
  2.8 5.3 %shard_map.144 = (bf16[8,128,512]{2,1,0:T(8,128)(2,1)}, bf16[32,128,512]{2,1,0:T(8,128)(2,1)}) custom-call(s32[32]{0:T(128)} %get-tuple-element.24.chosen_ref, bf16[8,128,512]{2,1,0:T(8,128)(2,1)} %inflow_ref.5, f32[1,512]{1,0:T(1,128)} %bitcast.11), custom_call_target="tpu_custom_call" | custom-call | tf_op jit(solution)/shard_map/pallas_call | solution.py:446
  8.1 0.0 copy-start.6
  8.1 0.0 copy-start.4
  8.1 0.0 copy-start.3
  8.1 0.0 copy-start.2
  8.1 0.0 copy-start
  8.1 0.0 copy-done.8
  8.1 10.0 %all-to-all-start = ((bf16[32,128,512]{2,1,0:T(8,128)(2,1)}), bf16[32,128,512]{2,1,0:T(8,128)(2,1)}, u32[]{:S(2)}, u32[]{:S(2)}) async-start(bf16[32,128,512]{2,1,0:T(8,128)(2,1)} %get-tuple-element.16), calls=%async_computation | async-start | bytes 8388608 | tf_op jit(solution)/shard_map/all_to_all | solution.py:457
  18.2 0.0 copy-done.6
  18.2 0.7 convert_reduce_fusion.1
  18.9 0.1 copy.28
  19.0 0.1 squeeze.4
  19.1 0.0 copy-done.4
  19.1 0.2 copy.29
  19.3 0.0 copy-done.3
  19.3 0.2 copy.30
  19.5 0.0 copy-done.2
  19.6 1.0 copy.32
  20.6 0.0 copy-done
  20.6 1.0 copy.31
  21.6 1.1 fusion
  22.7 1.3 copy.33.wkv_ref
  24.0 0.6 compare_select_fusion
  24.6 48.7 %all-to-all-done.up0_ref.up1_ref.up2_ref = bf16[32,128,512]{2,1,0:T(8,128)(2,1)} async-done(((bf16[32,128,512]{2,1,0:T(8,128)(2,1)}), bf16[32,128,512]{2,1,0:T(8,128)(2,1)}, u32[]{:S(2)}, u32[]{:S(2)}) %all-to-all-start) | async-done | bytes 4194336 | tf_op jit(solution)/shard_map/all_to_all | solution.py:457
  73.3 52.9 %shard_map.145 = (bf16[8,128,512]{2,1,0:T(8,128)(2,1)}, f32[8,128,512]{2,1,0:T(8,128)}, bf16[32,128,512]{2,1,0:T(8,128)(2,1)}, f32[4,512,512]{2,1,0:T(8,128)}) custom-call(s32[8]{0:T(128)} %copy-done.8, s32[24]{0:T(128)} %get-tuple-element.35.source_ref, s32[24]{0:T(128)} %get-tuple-element.34.target_ref, s32[8]{0:T(128)} %get-tuple-element.29.count_ref, ...), custom_call_target="tpu_custom_call" | custom-call | tf_op jit(solution)/shard_map/pallas_call | solution.py:467
  126.2 0.0 copy-start.1
  126.2 0.0 copy-start.5
  126.2 113.9 %shard_map.146 = (bf16[32,128,512]{2,1,0:T(8,128)(2,1)}, f32[2048,512]{1,0:T(8,128)}) custom-call(bf16[32,128,512]{2,1,0:T(8,128)(2,1)} %get-tuple-element.19.sent_ref, f32[2048,512]{1,0:T(8,128)} %bitcast.8), custom_call_target="tpu_custom_call" | custom-call | tf_op jit(solution)/shard_map/pallas_call | solution.py:389
  240.1 0.0 copy-done.1
  240.1 0.0 copy-done.5
  240.1 0.0 copy-start.7
  240.1 4.5 %add_reduce_fusion = (f32[512]{0:T(512)S(1)}, f32[512,512]{1,0:T(8,128)}, f32[512,512]{1,0:T(8,128)}, f32[512,512]{1,0:T(8,128)}, f32[512,512]{1,0:T(8,128)}) fusion(bf16[512,512]{1,0:T(8,128)(2,1)S(1)} %copy-done.3, bf16[512,512]{1,0:T(8,128)(2,1)S(1)} %copy-done.5, bf16[512,512]{1,0:T(8,128)(2,1)S(1)} %copy-done.1, f32[2048,512]{1,0:T(8,128)} %get-tuple-element.22), kind=kLoop, calls=%fused_computation.1 | loop fusion | flops 2358784 | bytes 9963520 | tf_op jit(solution)/shard_map/reduce_sum | solution.py:547
  244.6 0.0 copy-done.7
  244.6 0.6 div.3
  245.2 7.4 %shard_map.147 = bf16[8,128,512]{2,1,0:T(8,128)(2,1)} custom-call(s32[32]{0:T(128)} %get-tuple-element.24.chosen_ref, s32[32]{0:T(128)} %get-tuple-element.23.wanted_ref, f32[8,128,512]{2,1,0:T(8,128)} %get-tuple-element.18.grad_own_ref, bf16[32,128,512]{2,1,0:T(8,128)(2,1)} %get-tuple-element.21.returned_ref, bf16[8,128,512]{2,1,0:T(8,128)(2,1)} %inflow_ref.5, ...), custom_call_target="tpu_custom_call" | custom-call | tf_op jit(solution)/shard_map/pallas_call | solution.py:523
Async XLA Ops:
  1.4 6.8 %copy-start.8 = (s32[8]{0:T(128)}, s32[8]{0:T(128)S(1)}, u32[]{:S(2)}) copy-start(s32[8]{0:T(128)S(1)} %select_reduce_fusion.1.order_ref) | copy-start | bytes 100
  8.1 10.0 %copy-start.6 = (s32[8,32,3]{1,0,2:T(8,128)S(1)}, s32[8,32,3]{1,0,2:T(8,128)}, u32[]{:S(2)}) copy-start(s32[8,32,3]{1,0,2:T(8,128)} %param.16) | copy-start | bytes 9220
  8.1 11.0 %copy-start.4 = (bf16[512,512]{1,0:T(8,128)(2,1)S(1)}, bf16[512,512]{1,0:T(8,128)(2,1)}, u32[]{:S(2)}) copy-start(bf16[512,512]{1,0:T(8,128)(2,1)} %param.13) | copy-start | bytes 1572868
  8.1 11.2 %copy-start.3 = (bf16[512,512]{1,0:T(8,128)(2,1)S(1)}, bf16[512,512]{1,0:T(8,128)(2,1)}, u32[]{:S(2)}) copy-start(bf16[512,512]{1,0:T(8,128)(2,1)} %param.14) | copy-start | bytes 1572868
  8.1 11.4 %copy-start.2 = (bf16[512,512]{1,0:T(8,128)(2,1)S(1)}, bf16[512,512]{1,0:T(8,128)(2,1)}, u32[]{:S(2)}) copy-start(bf16[512,512]{1,0:T(8,128)(2,1)} %wo_ref.1) | copy-start | bytes 1572868
  8.1 12.4 %copy-start = (bf16[512,512]{1,0:T(8,128)(2,1)S(1)}, bf16[512,512]{1,0:T(8,128)(2,1)}, u32[]{:S(2)}) copy-start(bf16[512,512]{1,0:T(8,128)(2,1)} %wq_ref.1) | copy-start | bytes 1572868
  8.1 65.1 %all-to-all-start = ((bf16[32,128,512]{2,1,0:T(8,128)(2,1)}), bf16[32,128,512]{2,1,0:T(8,128)(2,1)}, u32[]{:S(2)}, u32[]{:S(2)}) async-start(bf16[32,128,512]{2,1,0:T(8,128)(2,1)} %get-tuple-element.16), calls=%async_computation | async-start | bytes 8388608 | tf_op jit(solution)/shard_map/all_to_all | solution.py:457
  126.2 113.9 %copy-start.1 = (bf16[512,512]{1,0:T(8,128)(2,1)S(1)}, bf16[512,512]{1,0:T(8,128)(2,1)}, u32[]{:S(2)}) copy-start(bf16[512,512]{1,0:T(8,128)(2,1)} %wq_ref.1) | copy-start | bytes 1572868
  126.2 113.9 %copy-start.5 = (bf16[512,512]{1,0:T(8,128)(2,1)S(1)}, bf16[512,512]{1,0:T(8,128)(2,1)}, u32[]{:S(2)}) copy-start(bf16[512,512]{1,0:T(8,128)(2,1)} %param.13) | copy-start | bytes 1572868
  240.1 4.5 %copy-start.7 = (f32[512]{0:T(512)S(1)}, f32[512]{0:T(512)}, u32[]{:S(2)}) copy-start(f32[512]{0:T(512)} %param.11) | copy-start | bytes 6148
